TPU v7x, 32 devices: a whole 2x2x4 slice. The times are simulated.
32 devices in a mesh: lat: 8 (over z, y), lon: 4 (over x, core).
Axes of the slice: x: 2, y: 2, z: 4, core: 2. Of those that a mesh axis runs over, the one named last changes fastest.
Arguments:
- pair_table: int32 [640], replicated, may hold values from 0 to 639, each once
- spectral: bfloat16 [640, 384, 1408], P('lat', 'lon'), may hold values from -0.071777344 to 0.071777344
- lat_basis: bfloat16 [640, 32, 1408], P('lat'), may hold values from -0.15625 to 0.15625
- in_weight: bfloat16 [192, 512], replicated, may hold values from -0.4375 to 0.4375
- in_bias: float32 [512], replicated, may hold values from -3 to 3
- out_weight: bfloat16 [512, 192], replicated, may hold values from -0.25 to 0.25
- out_bias: float32 [192], replicated, may hold values from -3 to 3
- cotangent: bfloat16 [64, 192, 2560], P('lat', None, 'lon'), may hold values from -0.08984375 to 0.08984375
Outputs:
- tendency: bfloat16 [64, 192, 2560], P('lat', None, 'lon')
- spectral_grad: bfloat16 [640, 384, 1408], P('lat', 'lon')
- in_weight_grad: float32 [192, 512], replicated
- in_bias_grad: float32 [512], replicated
- out_weight_grad: float32 [512, 192], replicated
- out_bias_grad: float32 [192], replicated
Inputs may be any that keep to these rules, and one draw needn't show every extreme that they name: `pair_table`: each pair number appears exactly once.
All inputs are finite; a program needn't handle non-finite values.
Results may differ from a plain program's by a relative error of at most 0.015.
Values may be sent and summed in bfloat16 or wider, within the bound.
No kernel may reach another device: no remote copies, remote signals or barrier semaphores. Data moves between devices by JAX's collectives and lax.ppermute only.
A program may use at most 256 MiB of HBM per device.

v0:
```python
import math
import jax
import jax.numpy as jnp
from jax import lax
from jax.sharding import PartitionSpec as P

TRUNC = 1279


def pair_masks(pair_ids, length):
    first_len = TRUNC + 1 - pair_ids
    position = jnp.arange(length, dtype=jnp.int32)[None, :]
    lower_part = position < first_len[:, None]
    upper_part = jnp.logical_and(position >= first_len[:, None], position < TRUNC + 2)
    offset = jnp.where(lower_part, position, position - first_len[:, None])
    parity = jnp.where(offset % 2 == 0, 1.0, -1.0).astype(jnp.float32)
    return (lower_part, upper_part, parity, first_len)


def wave_numbers(pair_ids):
    both = jnp.stack([pair_ids, TRUNC - pair_ids], axis=1)
    return both.reshape(-1)


def fourier_table(numbers, lon_total):
    step = 128 if lon_total % 128 == 0 else 1
    coarse = jnp.arange(lon_total // step, dtype=jnp.int32) * step
    fine = jnp.arange(step, dtype=jnp.int32)
    scale = 2.0 * math.pi / lon_total

    def angles(offsets):
        phase = numbers[:, None] * offsets[None, :] % lon_total
        angle = phase.astype(jnp.float32) * scale
        return (jnp.cos(angle), jnp.sin(angle))

    cos_a, sin_a = angles(coarse)
    cos_b, sin_b = angles(fine)
    cos_t = cos_a[:, :, None] * cos_b[:, None, :] - sin_a[:, :, None] * sin_b[:, None, :]
    sin_t = sin_a[:, :, None] * cos_b[:, None, :] + cos_a[:, :, None] * sin_b[:, None, :]
    count = numbers.shape[0]
    factor = jnp.where(numbers == 0, 1.0, 2.0).astype(jnp.float32)[:, None]
    return jnp.stack(
        [factor * cos_t.reshape(count, lon_total), -factor * sin_t.reshape(count, lon_total)],
        axis=1,
    ).astype(jnp.bfloat16)


def per_device(
    pair_table, spectral, lat_basis, in_weight, in_bias, out_weight, out_bias, cotangent
):
    pair_dev = spectral.shape[0]
    width_local = spectral.shape[1]
    lat_half = lat_basis.shape[1]
    band_rows = cotangent.shape[0]
    block_cols = cotangent.shape[2]
    lon_total = block_cols * lax.axis_size("lon")
    first_row = lax.axis_index("lat") * pair_dev
    local_ids = lax.dynamic_slice_in_dim(pair_table, first_row, pair_dev)
    lower_part, upper_part, parity, first_len = pair_masks(local_ids, spectral.shape[2])
    rows = jnp.concatenate([lat_basis, lat_basis * parity[:, None, :].astype(jnp.bfloat16)], axis=1)
    zero = jnp.zeros_like(rows)
    basis = jnp.stack(
        [
            jnp.where(lower_part[:, None, :], rows, zero),
            jnp.where(upper_part[:, None, :], rows, zero),
        ],
        axis=1,
    )
    lat_window = 2 * lat_half
    raw_waves = jnp.einsum(
        "pqlj,pkj->pqlk", basis, spectral, preferred_element_type=jnp.float32
    ).astype(jnp.bfloat16)
    waves = jnp.concatenate(
        [raw_waves[:, :, :lat_half], jnp.flip(raw_waves[:, :, lat_half:], axis=2)], axis=2
    )
    flat_waves = waves.reshape(2 * pair_dev, lat_window * width_local)
    band_waves = lax.all_to_all(flat_waves, "lat", split_axis=1, concat_axis=0, tiled=True)
    wave_count = band_waves.shape[0]
    coeff_grid = band_waves.reshape(wave_count, band_rows, width_local // 2, 2)
    numbers = wave_numbers(pair_table)
    full_table = fourier_table(numbers, lon_total)
    all_columns = jnp.einsum(
        "glkc,gcn->lkn", coeff_grid, full_table, preferred_element_type=jnp.float32
    ).astype(jnp.bfloat16)
    grid = lax.all_to_all(all_columns, "lon", split_axis=2, concat_axis=1, tiled=True)
    pre_act = (
        jnp.einsum("lkc,kh->lch", grid, in_weight, preferred_element_type=jnp.float32) + in_bias
    )
    activated, gelu_back = jax.vjp(jax.nn.gelu, pre_act)
    hidden = activated.astype(jnp.bfloat16)
    tendency = (
        jnp.einsum("lch,hk->lkc", hidden, out_weight, preferred_element_type=jnp.float32)
        + out_bias[None, :, None]
    ).astype(jnp.bfloat16)
    out_weight_part = jnp.einsum(
        "lch,lkc->kh", hidden, cotangent, preferred_element_type=jnp.float32
    )
    out_bias_part = jnp.sum(cotangent.astype(jnp.float32), axis=(0, 2))
    hidden_grad = jnp.einsum(
        "lkc,hk->lch", cotangent, out_weight, preferred_element_type=jnp.float32
    )
    pre_grad = gelu_back(hidden_grad)[0].astype(jnp.bfloat16)
    in_weight_part = jnp.einsum("lkc,lch->kh", grid, pre_grad, preferred_element_type=jnp.float32)
    in_bias_part = jnp.sum(pre_grad.astype(jnp.float32), axis=(0, 1))
    grid_grad = jnp.einsum(
        "lch,kh->lkc", pre_grad, in_weight, preferred_element_type=jnp.float32
    ).astype(jnp.bfloat16)
    channels, hid = in_weight.shape
    width = max(hid, channels)

    def widen(v):
        return jnp.pad(v, ((0, 0), (0, width - v.shape[1])))

    stacked = jnp.concatenate(
        [
            widen(in_weight_part),
            widen(out_weight_part),
            widen(in_bias_part[None, :]),
            widen(out_bias_part[None, :]),
        ],
        axis=0,
    )
    summed = lax.psum(stacked, ("lat", "lon"))
    in_weight_grad = summed[:channels, :hid]
    out_weight_grad = summed[channels : 2 * channels, :hid].T
    in_bias_grad = summed[2 * channels, :hid]
    out_bias_grad = summed[2 * channels + 1, :channels]
    level_rows = lax.all_to_all(grid_grad, "lon", split_axis=1, concat_axis=2, tiled=True)
    wave_grad = jnp.einsum(
        "gcn,lkn->glkc", full_table, level_rows, preferred_element_type=jnp.float32
    ).astype(jnp.bfloat16)
    flat_grad = wave_grad.reshape(wave_count, band_rows * width_local)
    pair_grad = lax.all_to_all(flat_grad, "lat", split_axis=0, concat_axis=1, tiled=True)
    pair_grad = pair_grad.reshape(pair_dev, 2, lat_window, width_local)
    pair_grad = jnp.concatenate(
        [pair_grad[:, :, :lat_half], jnp.flip(pair_grad[:, :, lat_half:], axis=2)], axis=2
    )
    spectral_grad = jnp.einsum(
        "pqlk,pqlj->pkj", pair_grad, basis, preferred_element_type=jnp.float32
    ).astype(jnp.bfloat16)
    return (tendency, spectral_grad, in_weight_grad, in_bias_grad, out_weight_grad, out_bias_grad)


def solution(mesh):
    placed = (
        P(),
        P("lat", "lon", None),
        P("lat", None, None),
        P(),
        P(),
        P(),
        P(),
        P("lat", None, "lon"),
    )
    return jax.shard_map(
        per_device,
        mesh=mesh,
        in_specs=placed,
        out_specs=(P("lat", None, "lon"), P("lat", "lon", None), P(), P(), P(), P()),
        check_vma=False,
    )
```

profile of v0, /device:TPU:1, one launch (start us, length us, event | category | flops | bytes accessed | tf_op | source)
XLA Modules:
  0.0 477.1 jit_solution(11046358141665475062)
XLA Ops:
  7.2 0.0 copy-start
  7.2 0.8 dynamic-slice_subtract_fusion
  8.0 0.3 select_convert_fusion
  8.3 0.0 slice-start
  8.4 0.2 iota_compare_fusion.2
  8.6 0.0 slice-start.1
  8.6 7.1 %multiply_bitcast_fusion = bf16[80,1,32,1408]{3,2,1,0:T(8,128)(2,1)} fusion(bf16[80,32,1408]{2,1,0:T(8,128)(2,1)} %param.10, bf16[80,1408]{1,0:T(8,128)(2,1)S(1)} %select_convert_fusion), kind=kLoop, calls=%fused_computation.25 | loop fusion | flops 3604480 | bytes 14643200 | tf_op jit(solution)/shard_map/concatenate | solution.py:60
  15.7 14.2 %broadcast_select_fusion.1 = (bf16[80,1,64,1408]{3,2,1,0:T(8,128)(2,1)}, bf16[80,1,64,1408]{3,2,1,0:T(8,128)(2,1)}) fusion(pred[80,1408]{1,0:T(8,128)(4,1)S(1)} %get-tuple-element.22, bf16[80,1,32,1408]{3,2,1,0:T(8,128)(2,1)} %multiply_bitcast_fusion, bf16[80,1,32,1408]{3,2,1,0:T(8,128)(2,1)S(1)} %bitcast.97, pred[80,1408]{1,0:T(8,128)(4,1)S(1)} %get-tuple-element.23), kind=kLoop, calls=%fused_computation.8 | loop fusion | flops 43253760 | bytes 43479040 | tf_op jit(solution)/shard_map/jit(_where)/select_n | solution.py:64
  29.8 20.0 %fusion.18 = bf16[80,2,64,96]{3,2,1,0:T(8,128)(2,1)} fusion(bf16[80,96,1408]{2,1,0:T(8,128)(2,1)} %param.9, bf16[80,1,64,1408]{3,2,1,0:T(8,128)(2,1)} %get-tuple-element.7, bf16[80,1,64,1408]{3,2,1,0:T(8,128)(2,1)} %get-tuple-element.6), kind=kOutput, calls=%fused_computation.36 | convolution fusion | flops 2783641600 | bytes 52428800 | tf_op jit(solution)/shard_map/pqlj,pkj->pqlk/dot_general | solution.py:70
  49.8 3.4 fusion.52
  53.2 2.6 rev.7
  55.7 2.5 pad_maximum_fusion.4
  58.3 0.0 copy-start.6
  58.3 3.1 all_to_all.50
  61.4 3.2 copy.25
  64.6 6.9 %all-to-all-start = ((bf16[160,8,768]{2,0,1:T(8,128)(2,1)}), bf16[160,8,768]{2,0,1:T(8,128)(2,1)S(1)}, u32[]{:S(2)}, u32[]{:S(2)}) async-start(bf16[160,8,768]{2,0,1:T(8,128)(2,1)} %copy.25), calls=%async_computation | async-start | bytes 3932160 | tf_op jit(solution)/shard_map/all_to_all | solution.py:77
  71.6 0.2 copy.27
  71.8 0.2 reshape.455
  72.0 2.6 fusion.29
  74.7 1.3 fusion.44
  75.9 13.6 %multiply_subtract_fusion = (f32[1280,20,128]{0,2,1:T(8,128)}, f32[1280,20,128]{0,2,1:T(8,128)}) fusion(f32[1280,128]{0,1:T(8,128)S(1)} %get-tuple-element.21, f32[1280,20]{0,1:T(8,128)} %get-tuple-element.17, f32[1280,128]{0,1:T(8,128)S(1)} %get-tuple-element.20, f32[1280,20]{0,1:T(8,128)} %get-tuple-element.16), kind=kLoop, calls=%fused_computation.13 | loop fusion | flops 19660800 | bytes 27729920 | tf_op jit(solution)/shard_map/sub | solution.py:38
  89.6 14.0 %copy.29 = f32[1280,1,2560]{2,0,1:T(8,128)} copy(f32[1280,1,2560]{0,2,1:T(8,128)} %bitcast.94) | data formatting | bytes 26214400 | tf_op jit(solution)/shard_map/add | solution.py:39
  103.6 14.0 %copy.28 = f32[1280,1,2560]{2,0,1:T(8,128)} copy(f32[1280,1,2560]{0,2,1:T(8,128)} %bitcast.93) | data formatting | bytes 26214400 | tf_op jit(solution)/shard_map/sub | solution.py:38
  117.5 13.9 %multiply_convert_fusion = (bf16[1280,1,2560]{2,0,1:T(8,128)(2,1)}, bf16[1280,1,2560]{2,0,1:T(8,128)(2,1)}) fusion(f32[1280,1,2560]{2,0,1:T(8,128)} %copy.29, f32[1280]{0:T(1024)S(1)} %get-tuple-element.19, f32[1280,1,2560]{2,0,1:T(8,128)} %copy.28, f32[1280]{0:T(1024)S(1)} %get-tuple-element.18), kind=kLoop, calls=%fused_computation.10 | loop fusion | flops 13107200 | bytes 39331840 | tf_op jit(solution)/shard_map/convert.1
  131.5 1.3 copy-done.1
  132.7 4.1 copy.26
  136.8 5.2 %reshape.454 = bf16[1280,8,48,2]{0,3,2,1:T(2,128)(2,1)} reshape(bf16[8,160,768]{1,0,2:T(8,128)(2,1)S(1)} %copy.26) | data formatting | bytes 3932160 | tf_op jit(solution)/shard_map/reshape | solution.py:79
  142.1 8.9 %fusion.12 = bf16[8,48,2560]{2,1,0:T(8,128)(2,1)S(1)} fusion(bf16[1280,1,2560]{2,0,1:T(8,128)(2,1)} %get-tuple-element.28, bf16[1280,1,2560]{2,0,1:T(8,128)(2,1)} %get-tuple-element.29, bf16[1280,8,48,2]{0,3,2,1:T(2,128)(2,1)} %reshape.454), kind=kOutput, calls=%fused_computation.27 | convolution fusion | flops 5040701440 | bytes 17039360 | tf_op jit(solution)/shard_map/glkc,gcn->lkn/dot_general | solution.py:82
  151.0 5.4 %copy.31 = bf16[8,48,2560]{1,0,2:T(8,128)(2,1)} copy(bf16[8,48,2560]{2,1,0:T(8,128)(2,1)S(1)} %fusion.12) | data formatting | bytes 3932160 | tf_op jit(solution)/shard_map/convert_element_type | solution.py:84
  156.4 8.8 %reshape.467 = bf16[4,2,122880]{2,1,0:T(2,128)(2,1)S(1)} reshape(bf16[2560,8,48]{2,1,0:T(8,128)(2,1)} %bitcast.98) | data formatting | bytes 3932160
  165.3 27.4 %all_to_all.68 = bf16[4,2,122880]{2,1,0:T(2,128)(2,1)} all-to-all(bf16[4,2,122880]{2,1,0:T(2,128)(2,1)S(1)} %reshape.467), channel_id=1, replica_groups=mesh['lat'=8,'lon'=4] {'lon'}, dimensions={0} | all-to-all | bytes 3932160 | tf_op jit(solution)/shard_map/all_to_all | solution.py:85
  192.7 7.1 %reshape.468 = bf16[2560,8,48]{2,1,0:T(8,128)(2,1)} reshape(bf16[4,2,122880]{2,1,0:T(2,128)(2,1)} %all_to_all.68) | data formatting | bytes 3932160
  199.8 5.7 %copy.32 = bf16[8,48,4,640]{3,1,2,0:T(8,128)(2,1)S(1)} copy(bf16[8,48,4,640]{1,0,3,2:T(8,128)(2,1)} %bitcast.99) | data formatting | bytes 3932160 | tf_op jit(solution)/shard_map/all_to_all | solution.py:85
  205.5 0.0 copy-start.3
  205.5 0.0 copy-start.7
  205.5 5.5 %multiply_convert_fusion.2 = (bf16[8,640,512]{2,1,0:T(8,128)(2,1)}, f32[8,640,512]{2,1,0:T(8,128)S(1)}) fusion(f32[512]{0:T(512)S(1)} %copy-done.8, bf16[8,192,640]{2,1,0:T(8,128)(2,1)S(1)} %bitcast.104, bf16[192,512]{1,0:T(8,128)(2,1)S(1)} %copy-done), kind=kOutput, calls=%fused_computation.22 | convolution fusion | flops 1032847360 | bytes 17893376 | tf_op jit(solution)/shard_map/lkc,kh->lch/dot_general | solution.py:87
  211.0 8.7 %convert_reduce_fusion = (f32[512]{0:T(512)S(1)}, bf16[8,640,512]{2,1,0:T(8,128)(2,1)S(1)}) fusion(f32[8,640,512]{2,1,0:T(8,128)S(1)} %get-tuple-element.25, f32[512]{0:T(512)S(1)} %copy-done.8, bf16[8,192,640]{2,1,0:T(8,128)(2,1)S(1)} %copy-done.3, bf16[512,192]{0,1:T(8,128)(2,1)S(1)} %copy-done.7), kind=kOutput, calls=%fused_computation.21 | convolution fusion | flops 1066925568 | bytes 17895424 | tf_op jit(solution)/shard_map/lkc,hk->lch/dot_general | solution.py:99
  219.7 1.9 convert_bitcast_fusion
  221.6 1.1 copy.33
  222.7 26.9 %all_to_all.69 = bf16[8,192,640]{2,0,1:T(8,128)(2,1)S(1)} all-to-all(bf16[8,192,640]{2,0,1:T(8,128)(2,1)S(1)} %copy.33), channel_id=1, replica_groups=mesh['lat'=8,'lon'=4] {'lon'}, dimensions={1} | all-to-all | bytes 3932160 | tf_op jit(solution)/shard_map/all_to_all | solution.py:128
  249.7 1.5 copy.45
  251.2 2.2 reshape.462
  253.4 9.0 %fusion.14 = bf16[1280,8,48,2]{0,2,3,1:T(8,128)(2,1)S(1)} fusion(bf16[1280,1,2560]{2,0,1:T(8,128)(2,1)} %get-tuple-element.28, bf16[1280,1,2560]{2,0,1:T(8,128)(2,1)} %get-tuple-element.29, bf16[8,48,2560,1]{2,1,0,3:T(8,128)(2,1)} %reshape.462), kind=kOutput, calls=%fused_computation.31 | convolution fusion | flops 5060362240 | bytes 17039360 | tf_op jit(solution)/shard_map/gcn,lkn->glkc/dot_general | solution.py:129
  262.4 2.8 copy.35
  265.2 6.4 %all_to_all.61 = bf16[8,160,768]{1,0,2:T(8,128)(2,1)S(1)} reshape(bf16[1280,8,48,2]{0,3,2,1:T(2,128)(2,1)} %copy.35) | data formatting | bytes 3932160 | tf_op jit(solution)/shard_map/all_to_all | solution.py:133
  271.6 3.2 copy.36
  274.8 5.7 %all-to-all-start.3 = ((bf16[8,160,768]{2,1,0:T(8,128)(2,1)}), bf16[8,160,768]{2,1,0:T(8,128)(2,1)S(1)}, u32[]{:S(2)}, u32[]{:S(2)}) async-start(bf16[8,160,768]{2,1,0:T(8,128)(2,1)} %copy.36), calls=%async_computation.3 | async-start | bytes 3932160 | tf_op jit(solution)/shard_map/all_to_all | solution.py:133
  280.6 0.3 all-reduce.3.cloned.1.call-start
  280.9 2.0 convert_reduce_fusion.1
  282.9 4.6 convolution_bitcast_fusion.1
  287.5 0.0 copy-start.9
  287.6 1.2 convolution_bitcast_fusion
  288.8 1.0 select_maximum_fusion
  289.8 0.0 all-reduce.3.cloned.1.call-update
  289.8 5.6 %fusion.23 = bf16[8,192,640]{2,1,0:T(8,128)(2,1)} fusion(f32[192]{0:T(256)S(1)} %copy-done.9, bf16[8,640,512]{2,1,0:T(8,128)(2,1)} %get-tuple-element.24, bf16[512,192]{0,1:T(8,128)(2,1)S(1)} %copy-done.7), kind=kOutput, calls=%fused_computation.41 | convolution fusion | flops 1008599040 | bytes 7406336 | tf_op jit(solution)/shard_map/lch,hk->lkc/dot_general | solution.py:92
  295.4 136.8 %all-reduce.3.cloned.1.call-done = f32[386,512]{1,0:T(8,128)} async-done(((f32[386,512]{1,0:T(8,128)}), f32[386,512]{1,0:T(8,128)}) %all-reduce.3.cloned.1.call-update) | async-done | bytes 790544 | tf_op jit(solution)/shard_map/psum | solution.py:123
  432.2 1.3 slice.37
  433.5 1.3 slice.39
  434.7 2.0 slice_bitcast_fusion
  436.8 2.4 copy.37
  439.1 4.6 reshape.456
  443.7 2.4 fusion.51
  446.1 3.4 rev.8
  449.5 20.5 %bitcast_convert_fusion = bf16[80,96,1408]{2,1,0:T(8,128)(2,1)} fusion(bf16[80,1,64,1408]{3,2,1,0:T(8,128)(2,1)} %get-tuple-element.7, bf16[80,1,64,1408]{3,2,1,0:T(8,128)(2,1)} %get-tuple-element.6, bf16[80,2,32,96]{3,2,1,0:T(8,128)(2,1)S(1)} %rev.8, bf16[80,2,32,96]{3,2,1,0:T(8,128)(2,1)} %get-tuple-element.8), kind=kOutput, calls=%fused_computation | convolution fusion | flops 2797404160 | bytes 52428800 | tf_op jit(solution)/shard_map/pqlk,pqlj->pkj/dot_general | solution.py:138
  (31 shorter events, 0.1 us)
Async XLA Ops:
  7.2 198.3 %copy-start = (bf16[192,512]{1,0:T(8,128)(2,1)S(1)}, bf16[192,512]{1,0:T(8,128)(2,1)}, u32[]{:S(2)}) copy-start(bf16[192,512]{1,0:T(8,128)(2,1)} %param.11) | copy-start | bytes 589828
  8.3 7.3 %slice-start = ((s8[7208960]{0:T(1024)(128)(4,1)}), s8[4194304]{0:T(1024)(128)(4,1)S(1)}, s32[]{:S(2)}) async-start(s8[7208960]{0:T(1024)(128)(4,1)} %bitcast.95), calls=%async_computation.5 | async-start | bytes 8388608
  8.6 7.1 %slice-start.1 = ((s8[7208960]{0:T(1024)(128)(4,1)}), s8[3014656]{0:T(1024)(128)(4,1)S(1)}, s32[]{:S(2)}) async-start(s8[7208960]{0:T(1024)(128)(4,1)} %bitcast.95), calls=%async_computation.6 | async-start | bytes 6029312
  58.3 13.3 %copy-start.6 = (s32[640]{0:T(1024)S(1)}, s32[640]{0:T(1024)}, u32[]{:S(2)}) copy-start(s32[640]{0:T(1024)} %param.8) | copy-start | bytes 7684
  64.6 66.8 %all-to-all-start = ((bf16[160,8,768]{2,0,1:T(8,128)(2,1)}), bf16[160,8,768]{2,0,1:T(8,128)(2,1)S(1)}, u32[]{:S(2)}, u32[]{:S(2)}) async-start(bf16[160,8,768]{2,0,1:T(8,128)(2,1)} %copy.25), calls=%async_computation | async-start | bytes 3932160 | tf_op jit(solution)/shard_map/all_to_all | solution.py:77
  131.5 1.3 copy-start.1
  192.7 12.8 %copy-start.8 = (f32[512]{0:T(512)S(1)}, f32[512]{0:T(512)}, u32[]{:S(2)}) copy-start(f32[512]{0:T(512)} %param.12) | copy-start | bytes 6148
  205.5 5.6 %copy-start.5 = (bf16[8,48,4,640]{3,1,2,0:T(8,128)(2,1)}, bf16[8,48,4,640]{3,1,2,0:T(8,128)(2,1)S(1)}, u32[]{:S(2)}) copy-start(bf16[8,48,4,640]{3,1,2,0:T(8,128)(2,1)S(1)} %copy.32) | copy-start | bytes 5898244
  205.5 5.5 %copy-start.3 = (bf16[8,192,640]{2,1,0:T(8,128)(2,1)S(1)}, bf16[8,192,640]{2,1,0:T(8,128)(2,1)}, u32[]{:S(2)}) copy-start(bf16[8,192,640]{2,1,0:T(8,128)(2,1)} %param.15) | copy-start | bytes 5898244
  205.5 5.5 %copy-start.7 = (bf16[512,192]{0,1:T(8,128)(2,1)S(1)}, bf16[512,192]{0,1:T(8,128)(2,1)}, u32[]{:S(2)}) copy-start(bf16[512,192]{0,1:T(8,128)(2,1)} %param.13) | copy-start | bytes 589828
  219.7 29.9 %copy-start.2 = (bf16[8,640,512]{2,1,0:T(8,128)(2,1)}, bf16[8,640,512]{2,1,0:T(8,128)(2,1)S(1)}, u32[]{:S(2)}) copy-start(bf16[8,640,512]{2,1,0:T(8,128)(2,1)S(1)} %get-tuple-element.27) | copy-start | bytes 15728644
  274.8 161.9 %all-to-all-start.3 = ((bf16[8,160,768]{2,1,0:T(8,128)(2,1)}), bf16[8,160,768]{2,1,0:T(8,128)(2,1)S(1)}, u32[]{:S(2)}, u32[]{:S(2)}) async-start(bf16[8,160,768]{2,1,0:T(8,128)(2,1)} %copy.36), calls=%async_computation.3 | async-start | bytes 3932160 | tf_op jit(solution)/shard_map/all_to_all | solution.py:133
  280.6 151.6 %all-reduce.3.cloned.1.call-start = ((), (), s32[]{:S(2)}) async-start(), calls=%async_computation.4 | async-start | bytes 1605632 | tf_op jit(solution)/shard_map/psum | solution.py:123
  280.9 6.7 %copy-start.4 = (bf16[8,192,640]{2,1,0:T(8,128)(2,1)S(1)}, bf16[8,192,640]{2,1,0:T(8,128)(2,1)}, u32[]{:S(2)}) copy-start(bf16[8,192,640]{2,1,0:T(8,128)(2,1)} %param.15) | copy-start | bytes 5898244
  280.9 6.7 %slice-start.2 = ((s8[5242880]{0:T(1024)(128)(4,1)}), s8[4194304]{0:T(1024)(128)(4,1)S(1)}, s32[]{:S(2)}) async-start(s8[5242880]{0:T(1024)(128)(4,1)} %bitcast.110), calls=%async_computation.7 | async-start | bytes 8388608
  282.9 4.6 slice-start.3
  287.5 2.3 copy-start.9
Sparse Core Ops, SparseCore 0:
  289.9 142.2 all-reduce.2
where the time goes:
time: 484 us; the launch traced here: 477 us
  waiting for transfers between devices  137 us (28%)
  local copies, waits for them, and re-layouts  113 us (23%)
  matrix products  85.8 us (18%)
  other arithmetic  59.6 us (12%)
  blocking collectives  54.4 us (11%)
  between operations  14.7 us (3%)
  starting transfers between devices  12.9 us (3%)
    psum x1, waiting for transfers between devices, per_device(): summed = lax.psum(stacked, ('lat', 'lon'))  137 us
    all_to_all x1, blocking collectives, per_device(): lax.all_to_all(all_columns, 'lon', split_axis=2, concat_axis=1, tiled=True)  27.4 us
    all_to_all x1, blocking collectives, per_device(): lax.all_to_all(grid_grad, 'lon', split_axis=1, concat_axis=2, tiled=True)  26.9 us
    dot_general x1, matrix products, per_device(): jnp.einsum('pqlk,pqlj->pkj', pair_grad, basis, preferred_element_type=jnp...  20.5 us
    dot_general x1, matrix products, per_device(): jnp.einsum('pqlj,pkj->pqlk', basis, spectral, preferred_element_type=jnp....  20 us
    unnamed x30, local copies, waits for them, and re-layouts  17.3 us
    select_n x1, other arithmetic, per_device(): jnp.where(lower_part[:, None, :], rows, zero)  14.2 us
    add x1, local copies, waits for them, and re-layouts, fourier_table(): sin_a[:, :, None] * cos_b[:, None, :]  14 us
  transfers between devices with their start and end apart: 3, of which 1 were waited for; matrix products, arithmetic and copies ran while one was open for 17% of the time, Pallas kernels for 0%

commit v1 on v0

--- a/solution.py
+++ b/solution.py
@@ -120,7 +120,7 @@
         ],
         axis=0,
     )
-    summed = lax.psum(stacked, ("lat", "lon"))
+    summed = lax.psum(lax.psum(stacked, "lon"), "lat")
     in_weight_grad = summed[:channels, :hid]
     out_weight_grad = summed[channels : 2 * channels, :hid].T
     in_bias_grad = summed[2 * channels, :hid]

time: 484 us -> 457 us (0.944)
  waiting for transfers between devices: 137 us -> 107 us
    psum x1 -> x2, waiting for transfers between devices: 137 us -> 107 us  [per_device(): summed = lax.psum(lax.psum(stacked, 'lon'), 'lat')]
  transfers between devices with their start and end apart: 3 -> 4, of which waited for: 1 -> 2; matrix products, arithmetic and copies ran while one was open for 17% -> 18% of each run, Pallas kernels for 0% -> 0%
where the time goes in v1:
time: 457 us; the launch traced here: 448 us
  local copies, waits for them, and re-layouts  113 us (25%)
  waiting for transfers between devices  107 us (23%)
  matrix products  85.8 us (19%)
  other arithmetic  59.6 us (13%)
  blocking collectives  54.4 us (12%)
  between operations  14.7 us (3%)
  starting transfers between devices  13 us (3%)
    psum x2, waiting for transfers between devices, per_device(): summed = lax.psum(lax.psum(stacked, 'lon'), 'lat')  107 us
    all_to_all x1, blocking collectives, per_device(): lax.all_to_all(all_columns, 'lon', split_axis=2, concat_axis=1, tiled=True)  27.4 us
    all_to_all x1, blocking collectives, per_device(): lax.all_to_all(grid_grad, 'lon', split_axis=1, concat_axis=2, tiled=True)  26.9 us
    dot_general x1, matrix products, per_device(): jnp.einsum('pqlk,pqlj->pkj', pair_grad, basis, preferred_element_type=jnp...  20.5 us
    dot_general x1, matrix products, per_device(): jnp.einsum('pqlj,pkj->pqlk', basis, spectral, preferred_element_type=jnp....  20 us
    unnamed x30, local copies, waits for them, and re-layouts  17.3 us
    select_n x1, other arithmetic, per_device(): jnp.where(lower_part[:, None, :], rows, zero)  14.2 us
    add x1, local copies, waits for them, and re-layouts, fourier_table(): sin_a[:, :, None] * cos_b[:, None, :]  14 us
  transfers between devices with their start and end apart: 4, of which 2 were waited for; matrix products, arithmetic and copies ran while one was open for 18% of the time, Pallas kernels for 0%

profile of v1, /device:TPU:1, one launch (start us, length us, event | category | flops | bytes accessed | tf_op | source)
XLA Modules:
  0.0 447.8 jit_solution(9319112335756062495)
XLA Ops:
  7.2 0.0 copy-start
  7.2 0.8 dynamic-slice_subtract_fusion
  8.0 0.3 select_convert_fusion
  8.3 0.0 slice-start
  8.4 0.2 iota_compare_fusion.2
  8.6 0.0 slice-start.1
  8.6 7.1 %multiply_bitcast_fusion = bf16[80,1,32,1408]{3,2,1,0:T(8,128)(2,1)} fusion(bf16[80,32,1408]{2,1,0:T(8,128)(2,1)} %param.10, bf16[80,1408]{1,0:T(8,128)(2,1)S(1)} %select_convert_fusion), kind=kLoop, calls=%fused_computation.25 | loop fusion | flops 3604480 | bytes 14643200 | tf_op jit(solution)/shard_map/concatenate | solution.py:60
  15.7 14.2 %broadcast_select_fusion.1 = (bf16[80,1,64,1408]{3,2,1,0:T(8,128)(2,1)}, bf16[80,1,64,1408]{3,2,1,0:T(8,128)(2,1)}) fusion(pred[80,1408]{1,0:T(8,128)(4,1)S(1)} %get-tuple-element.22, bf16[80,1,32,1408]{3,2,1,0:T(8,128)(2,1)} %multiply_bitcast_fusion, bf16[80,1,32,1408]{3,2,1,0:T(8,128)(2,1)S(1)} %bitcast.97, pred[80,1408]{1,0:T(8,128)(4,1)S(1)} %get-tuple-element.23), kind=kLoop, calls=%fused_computation.8 | loop fusion | flops 43253760 | bytes 43479040 | tf_op jit(solution)/shard_map/jit(_where)/select_n | solution.py:64
  29.8 20.0 %fusion.18 = bf16[80,2,64,96]{3,2,1,0:T(8,128)(2,1)} fusion(bf16[80,96,1408]{2,1,0:T(8,128)(2,1)} %param.9, bf16[80,1,64,1408]{3,2,1,0:T(8,128)(2,1)} %get-tuple-element.7, bf16[80,1,64,1408]{3,2,1,0:T(8,128)(2,1)} %get-tuple-element.6), kind=kOutput, calls=%fused_computation.36 | convolution fusion | flops 2783641600 | bytes 52428800 | tf_op jit(solution)/shard_map/pqlj,pkj->pqlk/dot_general | solution.py:70
  49.8 3.4 fusion.52
  53.2 2.6 rev.7
  55.7 2.5 pad_maximum_fusion.4
  58.3 0.0 copy-start.6
  58.3 3.1 all_to_all.50
  61.4 3.2 copy.25
  64.6 6.9 %all-to-all-start = ((bf16[160,8,768]{2,0,1:T(8,128)(2,1)}), bf16[160,8,768]{2,0,1:T(8,128)(2,1)S(1)}, u32[]{:S(2)}, u32[]{:S(2)}) async-start(bf16[160,8,768]{2,0,1:T(8,128)(2,1)} %copy.25), calls=%async_computation | async-start | bytes 3932160 | tf_op jit(solution)/shard_map/all_to_all | solution.py:77
  71.6 0.2 copy.27
  71.8 0.2 reshape.455
  72.0 2.6 fusion.29
  74.7 1.3 fusion.44
  75.9 13.6 %multiply_subtract_fusion = (f32[1280,20,128]{0,2,1:T(8,128)}, f32[1280,20,128]{0,2,1:T(8,128)}) fusion(f32[1280,128]{0,1:T(8,128)S(1)} %get-tuple-element.21, f32[1280,20]{0,1:T(8,128)} %get-tuple-element.17, f32[1280,128]{0,1:T(8,128)S(1)} %get-tuple-element.20, f32[1280,20]{0,1:T(8,128)} %get-tuple-element.16), kind=kLoop, calls=%fused_computation.13 | loop fusion | flops 19660800 | bytes 27729920 | tf_op jit(solution)/shard_map/sub | solution.py:38
  89.6 14.0 %copy.29 = f32[1280,1,2560]{2,0,1:T(8,128)} copy(f32[1280,1,2560]{0,2,1:T(8,128)} %bitcast.94) | data formatting | bytes 26214400 | tf_op jit(solution)/shard_map/add | solution.py:39
  103.6 14.0 %copy.28 = f32[1280,1,2560]{2,0,1:T(8,128)} copy(f32[1280,1,2560]{0,2,1:T(8,128)} %bitcast.93) | data formatting | bytes 26214400 | tf_op jit(solution)/shard_map/sub | solution.py:38
  117.5 13.9 %multiply_convert_fusion = (bf16[1280,1,2560]{2,0,1:T(8,128)(2,1)}, bf16[1280,1,2560]{2,0,1:T(8,128)(2,1)}) fusion(f32[1280,1,2560]{2,0,1:T(8,128)} %copy.29, f32[1280]{0:T(1024)S(1)} %get-tuple-element.19, f32[1280,1,2560]{2,0,1:T(8,128)} %copy.28, f32[1280]{0:T(1024)S(1)} %get-tuple-element.18), kind=kLoop, calls=%fused_computation.10 | loop fusion | flops 13107200 | bytes 39331840 | tf_op jit(solution)/shard_map/convert.1
  131.5 1.3 copy-done.1
  132.7 4.1 copy.26
  136.8 5.2 %reshape.454 = bf16[1280,8,48,2]{0,3,2,1:T(2,128)(2,1)} reshape(bf16[8,160,768]{1,0,2:T(8,128)(2,1)S(1)} %copy.26) | data formatting | bytes 3932160 | tf_op jit(solution)/shard_map/reshape | solution.py:79
  142.1 8.9 %fusion.12 = bf16[8,48,2560]{2,1,0:T(8,128)(2,1)S(1)} fusion(bf16[1280,1,2560]{2,0,1:T(8,128)(2,1)} %get-tuple-element.28, bf16[1280,1,2560]{2,0,1:T(8,128)(2,1)} %get-tuple-element.29, bf16[1280,8,48,2]{0,3,2,1:T(2,128)(2,1)} %reshape.454), kind=kOutput, calls=%fused_computation.27 | convolution fusion | flops 5040701440 | bytes 17039360 | tf_op jit(solution)/shard_map/glkc,gcn->lkn/dot_general | solution.py:82
  151.0 5.4 %copy.31 = bf16[8,48,2560]{1,0,2:T(8,128)(2,1)} copy(bf16[8,48,2560]{2,1,0:T(8,128)(2,1)S(1)} %fusion.12) | data formatting | bytes 3932160 | tf_op jit(solution)/shard_map/convert_element_type | solution.py:84
  156.4 8.8 %reshape.467 = bf16[4,2,122880]{2,1,0:T(2,128)(2,1)S(1)} reshape(bf16[2560,8,48]{2,1,0:T(8,128)(2,1)} %bitcast.98) | data formatting | bytes 3932160
  165.3 27.4 %all_to_all.68 = bf16[4,2,122880]{2,1,0:T(2,128)(2,1)} all-to-all(bf16[4,2,122880]{2,1,0:T(2,128)(2,1)S(1)} %reshape.467), channel_id=1, replica_groups=mesh['lat'=8,'lon'=4] {'lon'}, dimensions={0} | all-to-all | bytes 3932160 | tf_op jit(solution)/shard_map/all_to_all | solution.py:85
  192.7 7.1 %reshape.468 = bf16[2560,8,48]{2,1,0:T(8,128)(2,1)} reshape(bf16[4,2,122880]{2,1,0:T(2,128)(2,1)} %all_to_all.68) | data formatting | bytes 3932160
  199.8 5.7 %copy.32 = bf16[8,48,4,640]{3,1,2,0:T(8,128)(2,1)S(1)} copy(bf16[8,48,4,640]{1,0,3,2:T(8,128)(2,1)} %bitcast.99) | data formatting | bytes 3932160 | tf_op jit(solution)/shard_map/all_to_all | solution.py:85
  205.5 5.5 %multiply_convert_fusion.2 = (bf16[8,640,512]{2,1,0:T(8,128)(2,1)}, f32[8,640,512]{2,1,0:T(8,128)S(1)}) fusion(f32[512]{0:T(512)S(1)} %copy-done.8, bf16[8,192,640]{2,1,0:T(8,128)(2,1)S(1)} %bitcast.104, bf16[192,512]{1,0:T(8,128)(2,1)S(1)} %copy-done), kind=kOutput, calls=%fused_computation.22 | convolution fusion | flops 1032847360 | bytes 17893376 | tf_op jit(solution)/shard_map/lkc,kh->lch/dot_general | solution.py:87
  211.0 8.7 %convert_reduce_fusion = (f32[512]{0:T(512)S(1)}, bf16[8,640,512]{2,1,0:T(8,128)(2,1)S(1)}) fusion(f32[8,640,512]{2,1,0:T(8,128)S(1)} %get-tuple-element.25, f32[512]{0:T(512)S(1)} %copy-done.8, bf16[8,192,640]{2,1,0:T(8,128)(2,1)S(1)} %copy-done.3, bf16[512,192]{0,1:T(8,128)(2,1)S(1)} %copy-done.7), kind=kOutput, calls=%fused_computation.21 | convolution fusion | flops 1066925568 | bytes 17895424 | tf_op jit(solution)/shard_map/lkc,hk->lch/dot_general | solution.py:99
  219.7 1.9 convert_bitcast_fusion
  221.6 1.1 copy.33
  222.7 26.9 %all_to_all.69 = bf16[8,192,640]{2,0,1:T(8,128)(2,1)S(1)} all-to-all(bf16[8,192,640]{2,0,1:T(8,128)(2,1)S(1)} %copy.33), channel_id=1, replica_groups=mesh['lat'=8,'lon'=4] {'lon'}, dimensions={1} | all-to-all | bytes 3932160 | tf_op jit(solution)/shard_map/all_to_all | solution.py:128
  249.7 1.5 copy.45
  251.2 2.2 reshape.462
  253.4 9.0 %fusion.14 = bf16[1280,8,48,2]{0,2,3,1:T(8,128)(2,1)S(1)} fusion(bf16[1280,1,2560]{2,0,1:T(8,128)(2,1)} %get-tuple-element.28, bf16[1280,1,2560]{2,0,1:T(8,128)(2,1)} %get-tuple-element.29, bf16[8,48,2560,1]{2,1,0,3:T(8,128)(2,1)} %reshape.462), kind=kOutput, calls=%fused_computation.31 | convolution fusion | flops 5060362240 | bytes 17039360 | tf_op jit(solution)/shard_map/gcn,lkn->glkc/dot_general | solution.py:129
  262.4 2.8 copy.35
  265.2 6.4 %all_to_all.61 = bf16[8,160,768]{1,0,2:T(8,128)(2,1)S(1)} reshape(bf16[1280,8,48,2]{0,3,2,1:T(2,128)(2,1)} %copy.35) | data formatting | bytes 3932160 | tf_op jit(solution)/shard_map/all_to_all | solution.py:133
  271.6 3.2 copy.36
  274.8 5.7 %all-to-all-start.3 = ((bf16[8,160,768]{2,1,0:T(8,128)(2,1)}), bf16[8,160,768]{2,1,0:T(8,128)(2,1)S(1)}, u32[]{:S(2)}, u32[]{:S(2)}) async-start(bf16[8,160,768]{2,1,0:T(8,128)(2,1)} %copy.36), calls=%async_computation.3 | async-start | bytes 3932160 | tf_op jit(solution)/shard_map/all_to_all | solution.py:133
  280.6 0.0 all-reduce.4.cloned.1.call-start
  280.6 2.0 convert_reduce_fusion.1
  282.7 4.6 %convolution_bitcast_fusion.1 = f32[192,512]{1,0:T(8,128)S(1)} fusion(bf16[8,192,640]{2,1,0:T(8,128)(2,1)} %bitcast.105, bf16[8,640,512]{2,1,0:T(8,128)(2,1)} %copy-done.2), kind=kOutput, calls=%fused_computation.43 | convolution fusion | flops 1006632960 | bytes 7602176 | tf_op jit(solution)/shard_map/lkc,lch->kh/dot_general | solution.py:103
  287.3 1.2 convolution_bitcast_fusion
  288.5 0.9 select_maximum_fusion
  289.5 0.0 all-reduce.4.cloned.1.call-update
  289.5 0.3 all-reduce.6.cloned.1.call-start
  289.8 34.5 %all-reduce.4.cloned.1.call-done = f32[386,512]{1,0:T(8,128)} async-done(((f32[386,512]{1,0:T(8,128)}), f32[386,512]{1,0:T(8,128)}) %all-reduce.4.cloned.1.call-update) | async-done | bytes 790544 | tf_op jit(solution)/shard_map/psum | solution.py:123
  324.3 0.0 all-reduce.6.cloned.1.call-update
  324.4 5.6 %fusion.23 = bf16[8,192,640]{2,1,0:T(8,128)(2,1)} fusion(f32[192]{0:T(256)S(1)} %copy-done.9, bf16[8,640,512]{2,1,0:T(8,128)(2,1)} %get-tuple-element.24, bf16[512,192]{0,1:T(8,128)(2,1)S(1)} %copy-done.7), kind=kOutput, calls=%fused_computation.41 | convolution fusion | flops 1008599040 | bytes 7406336 | tf_op jit(solution)/shard_map/lch,hk->lkc/dot_general | solution.py:92
  330.0 72.9 %all-reduce.6.cloned.1.call-done = f32[386,512]{1,0:T(8,128)} async-done(((f32[386,512]{1,0:T(8,128)}), f32[386,512]{1,0:T(8,128)}) %all-reduce.6.cloned.1.call-update) | async-done | bytes 790544 | tf_op jit(solution)/shard_map/psum | solution.py:123
  402.9 1.3 slice.37
  404.2 1.3 slice.39
  405.5 2.0 slice_bitcast_fusion
  407.5 2.4 copy.37
  409.9 4.6 %reshape.456 = bf16[80,2,64,96]{3,2,1,0:T(8,128)(2,1)S(1)} reshape(bf16[160,8,768]{2,1,0:T(8,128)(2,1)} %copy.37) | data formatting | bytes 3932160 | tf_op jit(solution)/shard_map/reshape | solution.py:134
  414.4 2.4 fusion.51
  416.8 3.4 rev.8
  420.2 20.5 %bitcast_convert_fusion = bf16[80,96,1408]{2,1,0:T(8,128)(2,1)} fusion(bf16[80,1,64,1408]{3,2,1,0:T(8,128)(2,1)} %get-tuple-element.7, bf16[80,1,64,1408]{3,2,1,0:T(8,128)(2,1)} %get-tuple-element.6, bf16[80,2,32,96]{3,2,1,0:T(8,128)(2,1)S(1)} %rev.8, bf16[80,2,32,96]{3,2,1,0:T(8,128)(2,1)} %get-tuple-element.8), kind=kOutput, calls=%fused_computation | convolution fusion | flops 2797404160 | bytes 52428800 | tf_op jit(solution)/shard_map/pqlk,pqlj->pkj/dot_general | solution.py:138
  (34 shorter events, 0.1 us)
Async XLA Ops:
  7.2 198.3 %copy-start = (bf16[192,512]{1,0:T(8,128)(2,1)S(1)}, bf16[192,512]{1,0:T(8,128)(2,1)}, u32[]{:S(2)}) copy-start(bf16[192,512]{1,0:T(8,128)(2,1)} %param.11) | copy-start | bytes 589828
  8.3 7.3 %slice-start = ((s8[7208960]{0:T(1024)(128)(4,1)}), s8[4194304]{0:T(1024)(128)(4,1)S(1)}, s32[]{:S(2)}) async-start(s8[7208960]{0:T(1024)(128)(4,1)} %bitcast.95), calls=%async_computation.6 | async-start | bytes 8388608
  8.6 7.1 %slice-start.1 = ((s8[7208960]{0:T(1024)(128)(4,1)}), s8[3014656]{0:T(1024)(128)(4,1)S(1)}, s32[]{:S(2)}) async-start(s8[7208960]{0:T(1024)(128)(4,1)} %bitcast.95), calls=%async_computation.7 | async-start | bytes 6029312
  58.3 13.3 %copy-start.6 = (s32[640]{0:T(1024)S(1)}, s32[640]{0:T(1024)}, u32[]{:S(2)}) copy-start(s32[640]{0:T(1024)} %param.8) | copy-start | bytes 7684
  64.6 66.8 %all-to-all-start = ((bf16[160,8,768]{2,0,1:T(8,128)(2,1)}), bf16[160,8,768]{2,0,1:T(8,128)(2,1)S(1)}, u32[]{:S(2)}, u32[]{:S(2)}) async-start(bf16[160,8,768]{2,0,1:T(8,128)(2,1)} %copy.25), calls=%async_computation | async-start | bytes 3932160 | tf_op jit(solution)/shard_map/all_to_all | solution.py:77
  131.5 1.3 copy-start.1
  192.7 12.8 %copy-start.8 = (f32[512]{0:T(512)S(1)}, f32[512]{0:T(512)}, u32[]{:S(2)}) copy-start(f32[512]{0:T(512)} %param.12) | copy-start | bytes 6148
  205.5 5.6 %copy-start.5 = (bf16[8,48,4,640]{3,1,2,0:T(8,128)(2,1)}, bf16[8,48,4,640]{3,1,2,0:T(8,128)(2,1)S(1)}, u32[]{:S(2)}) copy-start(bf16[8,48,4,640]{3,1,2,0:T(8,128)(2,1)S(1)} %copy.32) | copy-start | bytes 5898244
  205.5 5.5 %copy-start.3 = (bf16[8,192,640]{2,1,0:T(8,128)(2,1)S(1)}, bf16[8,192,640]{2,1,0:T(8,128)(2,1)}, u32[]{:S(2)}) copy-start(bf16[8,192,640]{2,1,0:T(8,128)(2,1)} %param.15) | copy-start | bytes 5898244
  205.5 5.5 %copy-start.7 = (bf16[512,192]{0,1:T(8,128)(2,1)S(1)}, bf16[512,192]{0,1:T(8,128)(2,1)}, u32[]{:S(2)}) copy-start(bf16[512,192]{0,1:T(8,128)(2,1)} %param.13) | copy-start | bytes 589828
  219.7 29.9 %copy-start.2 = (bf16[8,640,512]{2,1,0:T(8,128)(2,1)}, bf16[8,640,512]{2,1,0:T(8,128)(2,1)S(1)}, u32[]{:S(2)}) copy-start(bf16[8,640,512]{2,1,0:T(8,128)(2,1)S(1)} %get-tuple-element.27) | copy-start | bytes 15728644
  274.8 132.7 %all-to-all-start.3 = ((bf16[8,160,768]{2,1,0:T(8,128)(2,1)}), bf16[8,160,768]{2,1,0:T(8,128)(2,1)S(1)}, u32[]{:S(2)}, u32[]{:S(2)}) async-start(bf16[8,160,768]{2,1,0:T(8,128)(2,1)} %copy.36), calls=%async_computation.3 | async-start | bytes 3932160 | tf_op jit(solution)/shard_map/all_to_all | solution.py:133
  280.6 43.8 %all-reduce.4.cloned.1.call-start = ((), (), s32[]{:S(2)}) async-start(), calls=%async_computation.4 | async-start | bytes 1605632 | tf_op jit(solution)/shard_map/psum | solution.py:123
  280.6 6.7 %copy-start.4 = (bf16[8,192,640]{2,1,0:T(8,128)(2,1)S(1)}, bf16[8,192,640]{2,1,0:T(8,128)(2,1)}, u32[]{:S(2)}) copy-start(bf16[8,192,640]{2,1,0:T(8,128)(2,1)} %param.15) | copy-start | bytes 5898244
  280.6 6.7 %slice-start.2 = ((s8[5242880]{0:T(1024)(128)(4,1)}), s8[4194304]{0:T(1024)(128)(4,1)S(1)}, s32[]{:S(2)}) async-start(s8[5242880]{0:T(1024)(128)(4,1)} %bitcast.110), calls=%async_computation.8 | async-start | bytes 8388608
  282.7 4.6 %slice-start.3 = ((s8[5242880]{0:T(1024)(128)(4,1)}), s8[1048576]{0:T(1024)(128)(4,1)S(1)}, s32[]{:S(2)}) async-start(s8[5242880]{0:T(1024)(128)(4,1)} %bitcast.110), calls=%async_computation.9 | async-start | bytes 2097152
  287.3 37.1 %copy-start.9 = (f32[192]{0:T(256)S(1)}, f32[192]{0:T(256)}, u32[]{:S(2)}) copy-start(f32[192]{0:T(256)} %param.14) | copy-start | bytes 2308
  289.5 113.4 %all-reduce.6.cloned.1.call-start = ((), (), s32[]{:S(2)}) async-start(), calls=%async_computation.5 | async-start | bytes 1605632 | tf_op jit(solution)/shard_map/psum | solution.py:123
Sparse Core Ops, SparseCore 0:
  289.6 34.6 all-reduce.3
  327.8 75.0 all-reduce.5
